TPU v7x, 32 devices: a whole 2x2x4 slice. The times are simulated.
32 devices in a mesh: row: 8 (over y, x, core), col: 4 (over z).
Axes of the slice: x: 2, y: 2, z: 4, core: 2. Of those that a mesh axis runs over, the one named last changes fastest.
Arguments:
- mixture_fractions: float32 [54, 64, 512], P(None, 'row', 'col'), may hold values from -6 to 6
- spreading_coefficient: float32 [64, 512], P('row', 'col'), may hold values from 0.02 to 0.12
- flow_speed_vector: float32 [2, 64, 512], P(None, 'row', 'col'), may hold values from -0.15 to 0.15
- thermal_state: float32 [64, 512], P('row', 'col'), may hold values from -6 to 6
- chemistry_active_indicator: int32 [64, 512], P('row', 'col'), may hold values from 0 to 1, as said below
- entry_level_matrix: bfloat16 [256, 55], replicated, may hold values from -0.875 to 0.875
- entry_level_offset: float32 [256], replicated, may hold values from -3 to 3
- hidden_level_matrix: bfloat16 [256, 256], replicated, may hold values from -0.375 to 0.375
- hidden_level_offset: float32 [256], replicated, may hold values from -3 to 3
- final_level_matrix: bfloat16 [54, 256], replicated, may hold values from -0.375 to 0.375
- final_level_offset: float32 [54], replicated, may hold values from -3 to 3
Outputs:
- species_next: float32 [54, 64, 512], P(None, 'row', 'col')
Inputs may be any that keep to these rules, and one draw needn't show every extreme that they name: `chemistry_active_indicator`: split the grid into tiles of 8 x 128 cells and bands of 8 rows. Every tile holds at most 384 flagged cells, and in every band some tile holds exactly 384; every band holds exactly 512 flagged cells.
All inputs are finite; a program needn't handle non-finite values.
Results may differ from a plain program's by a relative error of at most 0.0003.
Values sent between devices are 32-bit elements; how exact they have to be, the bound alone decides.
A program may use at most 64 MiB of HBM per device.

v0:
```python
import jax
import jax.numpy as jnp
from jax import lax
from jax.sharding import PartitionSpec as P

SUBSTEPS = 8
TRANSPORT_STEPS = 3


time_step = 1.0
chem_step = 0.0625


def extended(array, sides, width):
    for axis, dim in sides:
        devices, length = (lax.axis_size(axis), array.shape[dim])
        up = [(i, (i + 1) % devices) for i in range(devices - 1)]
        down = [(j, i) for i, j in up]
        last = lax.slice_in_dim(array, length - width, length, axis=dim)
        initial = lax.slice_in_dim(array, 0, width, axis=dim)
        before = lax.ppermute(last, axis, up)
        after = lax.ppermute(initial, axis, down)
        array = jnp.concatenate([before, array, after], axis=dim)
    return array


def advance(padded, pad_diff, speed_cols, speed_rows):
    left_vals = padded[..., 1:-1, :-1]
    right_vals = padded[..., 1:-1, 1:]
    face_diff = 0.5 * (pad_diff[1:-1, :-1] + pad_diff[1:-1, 1:])
    face_speed = 0.5 * (speed_cols[1:-1, :-1] + speed_cols[1:-1, 1:])
    flux_cols = face_diff * (right_vals - left_vals) - (
        jnp.maximum(face_speed, 0.0) * left_vals + jnp.minimum(face_speed, 0.0) * right_vals
    )
    lower_vals = padded[..., :-1, 1:-1]
    upper_vals = padded[..., 1:, 1:-1]
    face_diff = 0.5 * (pad_diff[:-1, 1:-1] + pad_diff[1:, 1:-1])
    face_speed = 0.5 * (speed_rows[:-1, 1:-1] + speed_rows[1:, 1:-1])
    flux_rows = face_diff * (upper_vals - lower_vals) - (
        jnp.maximum(face_speed, 0.0) * lower_vals + jnp.minimum(face_speed, 0.0) * upper_vals
    )
    change = (
        flux_cols[..., 1:] - flux_cols[..., :-1] + flux_rows[..., 1:, :] - flux_rows[..., :-1, :]
    )
    return padded[..., 1:-1, 1:-1] + time_step * change


def network(
    inputs,
    entry_level_matrix,
    entry_level_offset,
    hidden_level_matrix,
    hidden_level_offset,
    final_level_matrix,
    final_level_offset,
):
    hidden = jnp.tanh(
        jnp.dot(entry_level_matrix, inputs, preferred_element_type=jnp.float32)
        + entry_level_offset[:, None]
    ).astype(jnp.bfloat16)
    hidden = jnp.tanh(
        jnp.dot(hidden_level_matrix, hidden, preferred_element_type=jnp.float32)
        + hidden_level_offset[:, None]
    ).astype(jnp.bfloat16)
    return (
        jnp.dot(final_level_matrix, hidden, preferred_element_type=jnp.float32)
        + final_level_offset[:, None]
    )


def integrate(
    state,
    heat,
    entry_level_matrix,
    entry_level_offset,
    hidden_level_matrix,
    hidden_level_offset,
    final_level_matrix,
    final_level_offset,
):
    total = jnp.zeros(state.shape, jnp.float32)
    for index in range(SUBSTEPS):
        inputs = jnp.concatenate([state + chem_step * total, heat[None]], 0).astype(jnp.bfloat16)
        total = total + network(
            inputs,
            entry_level_matrix,
            entry_level_offset,
            hidden_level_matrix,
            hidden_level_offset,
            final_level_matrix,
            final_level_offset,
        )
    return chem_step * total


def species_halo(field):
    return extended(field, (("row", 1), ("col", 2)), 1)


def shards(
    mixture_fractions,
    spreading_coefficient,
    flow_speed_vector,
    thermal_state,
    chemistry_active_indicator,
    entry_level_matrix,
    entry_level_offset,
    hidden_level_matrix,
    hidden_level_offset,
    final_level_matrix,
    final_level_offset,
):
    species_count, tile_rows, tile_cols = mixture_fractions.shape
    cell_total = tile_rows * tile_cols
    cell_capacity = 3 * (cell_total // 8)
    coefficients = jnp.concatenate([spreading_coefficient[None], flow_speed_vector], 0)
    coefficients = extended(coefficients, (("row", 1), ("col", 2)), 1)
    carried_quantity = mixture_fractions
    for section in range(TRANSPORT_STEPS):
        padded = species_halo(carried_quantity)
        carried_quantity = advance(padded, coefficients[0], coefficients[1], coefficients[2])
    predictor_vector = jnp.concatenate([carried_quantity, thermal_state[None]], 0).reshape(
        species_count + 1, cell_total
    )
    active = chemistry_active_indicator.reshape(-1)
    place = jnp.cumsum(active) - 1
    slot_cell = (
        jnp.zeros((cell_capacity + 1,), jnp.int32)
        .at[jnp.where(active == 1, place, cell_capacity)]
        .set(jnp.arange(cell_total, dtype=jnp.int32))[:cell_capacity]
    )
    active_total = jnp.sum(active)
    filled = jnp.arange(cell_capacity, dtype=jnp.int32) < active_total
    gathered = predictor_vector[:, slot_cell]
    slot_rates = integrate(
        gathered[:species_count],
        gathered[species_count],
        entry_level_matrix,
        entry_level_offset,
        hidden_level_matrix,
        hidden_level_offset,
        final_level_matrix,
        final_level_offset,
    )
    target = jnp.where(filled, slot_cell, cell_total)
    increments = (
        jnp.zeros((species_count, cell_total + 1), jnp.float32)
        .at[:, target]
        .add(slot_rates)[:, :cell_total]
    )
    species_next = carried_quantity.reshape(species_count, cell_total) + increments
    return species_next.reshape(species_count, tile_rows, tile_cols)


def solution(mesh):
    in_specs = (
        P(None, "row", "col"),
        P("row", "col"),
        P(None, "row", "col"),
        P("row", "col"),
        P("row", "col"),
        P(),
        P(),
        P(),
        P(),
        P(),
        P(),
    )
    out_specs = P(None, "row", "col")
    return jax.shard_map(shards, mesh=mesh, in_specs=in_specs, out_specs=out_specs, check_vma=False)
```

profile of v0, /device:TPU:27, one launch (start us, length us, event | category | flops | bytes accessed | tf_op | source)
XLA Modules:
  0.0 105.1 jit_solution(13170058494623739615)
XLA Ops:
  0.8 3.7 %collective-permute-start = (f32[3,1,128]{2,1,0:T(1,128)S(1)}, f32[3,1,128]{2,1,0:T(1,128)S(1)}, u32[]{:S(2)}, u32[]{:S(2)}) collective-permute-start(f32[3,1,128]{2,1,0:T(1,128)S(1)} %get-tuple-element.26), channel_id=1, source_target_pairs={{0,4},{4,8},{8,12},{12,16},{16,20},{20,24},{24,28},{1,5},{5,9},{9,... | collective-permute-start | bytes 4616 | tf_op jit(solution)/shard_map/ppermute | solution.py:21
  4.5 1.9 %collective-permute-start.1 = (f32[3,1,128]{2,1,0:T(1,128)S(1)}, f32[3,1,128]{2,1,0:T(1,128)S(1)}, u32[]{:S(2)}, u32[]{:S(2)}) collective-permute-start(f32[3,1,128]{2,1,0:T(1,128)S(1)} %get-tuple-element.27), channel_id=1, source_target_pairs={{4,0},{8,4},{12,8},{16,12},{20,16},{24,20},{28,24},{5,1},{9,5},{13... | collective-permute-start | bytes 4616 | tf_op jit(solution)/shard_map/ppermute | solution.py:22
  7.5 4.5 %collective-permute-start.4 = (f32[54,1,128]{2,1,0:T(1,128)S(1)}, f32[54,1,128]{2,1,0:T(1,128)S(1)}, u32[]{:S(2)}, u32[]{:S(2)}) collective-permute-start(f32[54,1,128]{2,1,0:T(1,128)S(1)} %get-tuple-element.15), channel_id=1, source_target_pairs={{0,4},{4,8},{8,12},{12,16},{16,20},{20,24},{24,28},{1,5},{5,9},{9,... | collective-permute-start | bytes 82952 | tf_op jit(solution)/shard_map/ppermute | solution.py:21
  12.0 1.9 %collective-permute-start.5 = (f32[54,1,128]{2,1,0:T(1,128)S(1)}, f32[54,1,128]{2,1,0:T(1,128)S(1)}, u32[]{:S(2)}, u32[]{:S(2)}) collective-permute-start(f32[54,1,128]{2,1,0:T(1,128)S(1)} %get-tuple-element.16), channel_id=1, source_target_pairs={{4,0},{8,4},{12,8},{16,12},{20,16},{24,20},{28,24},{5,1},{9,5},{13... | collective-permute-start | bytes 82952 | tf_op jit(solution)/shard_map/ppermute | solution.py:22
  16.2 1.4 %collective-permute-start.2 = (f32[3,10,1]{2,1,0:T(8,128)S(1)}, f32[3,10,1]{2,1,0:T(8,128)S(1)}, u32[]{:S(2)}, u32[]{:S(2)}) collective-permute-start(f32[3,10,1]{2,1,0:T(8,128)S(1)} %get-tuple-element.20), channel_id=1, source_target_pairs={{0,1},{1,2},{2,3},{4,5},{5,6},{6,7},{8,9},{9,10},{10,11},{12,13},{... | collective-permute-start | bytes 368 | tf_op jit(solution)/shard_map/ppermute | solution.py:21
  17.7 4.0 %collective-permute-start.3 = (f32[3,10,1]{2,1,0:T(8,128)S(1)}, f32[3,10,1]{2,1,0:T(8,128)S(1)}, u32[]{:S(2)}, u32[]{:S(2)}) collective-permute-start(f32[3,10,1]{2,1,0:T(8,128)S(1)} %get-tuple-element.21), channel_id=1, source_target_pairs={{1,0},{2,1},{3,2},{5,4},{6,5},{7,6},{9,8},{10,9},{11,10},{13,12},{... | collective-permute-start | bytes 368 | tf_op jit(solution)/shard_map/ppermute | solution.py:22
  21.7 4.3 %scatter_custom_fusion = s32[385]{0:T(512)S(1)} fusion(s32[1024]{0:T(1024)S(1)} %bitcast.94, s32[1024]{0:T(1024)S(1)} %iota.7, s32[]{:T(128)} %constant.12.clone.1), kind=kCustom, calls=%fused_computation.194 | custom fusion | bytes 1544 | tf_op jit(solution)/shard_map/scatter | solution.py:130
  26.6 2.1 %collective-permute-start.6 = (f32[54,10,1]{2,1,0:T(8,128)S(1)}, f32[54,10,1]{2,1,0:T(8,128)S(1)}, u32[]{:S(2)}, u32[]{:S(2)}) collective-permute-start(f32[54,10,1]{2,1,0:T(8,128)S(1)} %get-tuple-element.10), channel_id=1, source_target_pairs={{1,0},{2,1},{3,2},{5,4},{6,5},{7,6},{9,8},{10,9},{11,10},{13,12},{... | collective-permute-start | bytes 6488 | tf_op jit(solution)/shard_map/ppermute | solution.py:22
  30.3 7.6 %collective-permute-done.6 = f32[54,10,1]{2,1,0:T(8,128)S(1)} collective-permute-done((f32[54,10,1]{2,1,0:T(8,128)S(1)}, f32[54,10,1]{2,1,0:T(8,128)S(1)}, u32[]{:S(2)}, u32[]{:S(2)}) %collective-permute-start.6) | collective-permute-done | bytes 2192 | tf_op jit(solution)/shard_map/ppermute | solution.py:22
  37.9 3.9 %collective-permute-done.7 = f32[54,10,1]{2,1,0:T(8,128)S(1)} collective-permute-done((f32[54,10,1]{2,1,0:T(8,128)S(1)}, f32[54,10,1]{2,1,0:T(8,128)S(1)}, u32[]{:S(2)}, u32[]{:S(2)}) %collective-permute-start.7) | collective-permute-done | bytes 2192 | tf_op jit(solution)/shard_map/ppermute | solution.py:21
  42.3 3.5 %collective-permute-start.8 = (f32[54,1,128]{2,1,0:T(1,128)S(1)}, f32[54,1,128]{2,1,0:T(1,128)S(1)}, u32[]{:S(2)}, u32[]{:S(2)}) collective-permute-start(f32[54,1,128]{2,1,0:T(1,128)S(1)} %get-tuple-element.13), channel_id=1, source_target_pairs={{0,4},{4,8},{8,12},{12,16},{16,20},{20,24},{24,28},{1,5},{5,9},{9,... | collective-permute-start | bytes 82952 | tf_op jit(solution)/shard_map/ppermute | solution.py:21
  45.8 1.9 %collective-permute-start.9 = (f32[54,1,128]{2,1,0:T(1,128)S(1)}, f32[54,1,128]{2,1,0:T(1,128)S(1)}, u32[]{:S(2)}, u32[]{:S(2)}) collective-permute-start(f32[54,1,128]{2,1,0:T(1,128)S(1)} %get-tuple-element.14), channel_id=1, source_target_pairs={{4,0},{8,4},{12,8},{16,12},{20,16},{24,20},{28,24},{5,1},{9,5},{13... | collective-permute-start | bytes 82952 | tf_op jit(solution)/shard_map/ppermute | solution.py:22
  48.4 3.5 %collective-permute-done.9 = f32[54,1,128]{2,1,0:T(1,128)S(1)} collective-permute-done((f32[54,1,128]{2,1,0:T(1,128)S(1)}, f32[54,1,128]{2,1,0:T(1,128)S(1)}, u32[]{:S(2)}, u32[]{:S(2)}) %collective-permute-start.9) | collective-permute-done | bytes 27680 | tf_op jit(solution)/shard_map/ppermute | solution.py:22
  52.2 2.1 %collective-permute-start.10 = (f32[54,10,1]{2,1,0:T(8,128)S(1)}, f32[54,10,1]{2,1,0:T(8,128)S(1)}, u32[]{:S(2)}, u32[]{:S(2)}) collective-permute-start(f32[54,10,1]{2,1,0:T(8,128)S(1)} %get-tuple-element.8), channel_id=1, source_target_pairs={{1,0},{2,1},{3,2},{5,4},{6,5},{7,6},{9,8},{10,9},{11,10},{13,12},{... | collective-permute-start | bytes 6488 | tf_op jit(solution)/shard_map/ppermute | solution.py:22
  54.3 1.3 %collective-permute-start.11 = (f32[54,10,1]{2,1,0:T(8,128)S(1)}, f32[54,10,1]{2,1,0:T(8,128)S(1)}, u32[]{:S(2)}, u32[]{:S(2)}) collective-permute-start(f32[54,10,1]{2,1,0:T(8,128)S(1)} %get-tuple-element.7), channel_id=1, source_target_pairs={{0,1},{1,2},{2,3},{4,5},{5,6},{6,7},{8,9},{9,10},{10,11},{12,13},{... | collective-permute-start | bytes 6488 | tf_op jit(solution)/shard_map/ppermute | solution.py:21
  55.7 7.9 %collective-permute-done.10 = f32[54,10,1]{2,1,0:T(8,128)S(1)} collective-permute-done((f32[54,10,1]{2,1,0:T(8,128)S(1)}, f32[54,10,1]{2,1,0:T(8,128)S(1)}, u32[]{:S(2)}, u32[]{:S(2)}) %collective-permute-start.10) | collective-permute-done | bytes 2192 | tf_op jit(solution)/shard_map/ppermute | solution.py:22
  63.6 4.1 %collective-permute-done.11 = f32[54,10,1]{2,1,0:T(8,128)S(1)} collective-permute-done((f32[54,10,1]{2,1,0:T(8,128)S(1)}, f32[54,10,1]{2,1,0:T(8,128)S(1)}, u32[]{:S(2)}, u32[]{:S(2)}) %collective-permute-start.11) | collective-permute-done | bytes 2192 | tf_op jit(solution)/shard_map/ppermute | solution.py:21
  68.2 2.0 %collective-permute-start.12 = (f32[54,1,128]{2,1,0:T(1,128)S(1)}, f32[54,1,128]{2,1,0:T(1,128)S(1)}, u32[]{:S(2)}, u32[]{:S(2)}) collective-permute-start(f32[54,1,128]{2,1,0:T(1,128)S(1)} %get-tuple-element.11), channel_id=1, source_target_pairs={{0,4},{4,8},{8,12},{12,16},{16,20},{20,24},{24,28},{1,5},{5,9},{9,... | collective-permute-start | bytes 82952 | tf_op jit(solution)/shard_map/ppermute | solution.py:21
  70.3 2.3 %collective-permute-start.13 = (f32[54,1,128]{2,1,0:T(1,128)S(1)}, f32[54,1,128]{2,1,0:T(1,128)S(1)}, u32[]{:S(2)}, u32[]{:S(2)}) collective-permute-start(f32[54,1,128]{2,1,0:T(1,128)S(1)} %get-tuple-element.12), channel_id=1, source_target_pairs={{4,0},{8,4},{12,8},{16,12},{20,16},{24,20},{28,24},{5,1},{9,5},{13... | collective-permute-start | bytes 82952 | tf_op jit(solution)/shard_map/ppermute | solution.py:22
  73.5 2.9 %collective-permute-done.13 = f32[54,1,128]{2,1,0:T(1,128)S(1)} collective-permute-done((f32[54,1,128]{2,1,0:T(1,128)S(1)}, f32[54,1,128]{2,1,0:T(1,128)S(1)}, u32[]{:S(2)}, u32[]{:S(2)}) %collective-permute-start.13) | collective-permute-done | bytes 27680 | tf_op jit(solution)/shard_map/ppermute | solution.py:22
  76.6 1.9 %collective-permute-start.14 = (f32[54,10,1]{2,1,0:T(8,128)S(1)}, f32[54,10,1]{2,1,0:T(8,128)S(1)}, u32[]{:S(2)}, u32[]{:S(2)}) collective-permute-start(f32[54,10,1]{2,1,0:T(8,128)S(1)} %get-tuple-element.6), channel_id=1, source_target_pairs={{1,0},{2,1},{3,2},{5,4},{6,5},{7,6},{9,8},{10,9},{11,10},{13,12},{... | collective-permute-start | bytes 6488 | tf_op jit(solution)/shard_map/ppermute | solution.py:22
  80.0 8.3 %collective-permute-done.14 = f32[54,10,1]{2,1,0:T(8,128)S(1)} collective-permute-done((f32[54,10,1]{2,1,0:T(8,128)S(1)}, f32[54,10,1]{2,1,0:T(8,128)S(1)}, u32[]{:S(2)}, u32[]{:S(2)}) %collective-permute-start.14) | collective-permute-done | bytes 2192 | tf_op jit(solution)/shard_map/ppermute | solution.py:22
  88.3 4.3 %collective-permute-done.15 = f32[54,10,1]{2,1,0:T(8,128)S(1)} collective-permute-done((f32[54,10,1]{2,1,0:T(8,128)S(1)}, f32[54,10,1]{2,1,0:T(8,128)S(1)}, u32[]{:S(2)}, u32[]{:S(2)}) %collective-permute-start.15) | collective-permute-done | bytes 2192 | tf_op jit(solution)/shard_map/ppermute | solution.py:21
  101.0 3.2 %scatter_custom_fusion.1 = f32[54,1025]{0,1:T(8,128)S(1)} fusion(s32[384]{0:T(512)S(1)} %get-tuple-element.31, f32[384,54]{1,0:T(8,128)S(1)} %copy.30, f32[]{:T(128)} %constant.11.clone.1), kind=kCustom, calls=%fused_computation.115 | custom fusion | flops 20736 | bytes 221404 | tf_op jit(solution)/shard_map/scatter-add | solution.py:149
  (93 shorter events, 20.1 us)
Async XLA Ops:
  0.0 94.8 %copy-start = (bf16[256,256]{1,0:T(8,128)(2,1)S(1)}, bf16[256,256]{1,0:T(8,128)(2,1)}, u32[]{:S(2)}) copy-start(bf16[256,256]{1,0:T(8,128)(2,1)} %param.18) | copy-start | bytes 393220
  0.8 15.3 %collective-permute-start = (f32[3,1,128]{2,1,0:T(1,128)S(1)}, f32[3,1,128]{2,1,0:T(1,128)S(1)}, u32[]{:S(2)}, u32[]{:S(2)}) collective-permute-start(f32[3,1,128]{2,1,0:T(1,128)S(1)} %get-tuple-element.26), channel_id=1, source_target_pairs={{0,4},{4,8},{8,12},{12,16},{16,20},{20,24},{24,28},{1,5},{5,9},{9,... | collective-permute-start | bytes 4616 | tf_op jit(solution)/shard_map/ppermute | solution.py:21
  4.5 11.7 %collective-permute-start.1 = (f32[3,1,128]{2,1,0:T(1,128)S(1)}, f32[3,1,128]{2,1,0:T(1,128)S(1)}, u32[]{:S(2)}, u32[]{:S(2)}) collective-permute-start(f32[3,1,128]{2,1,0:T(1,128)S(1)} %get-tuple-element.27), channel_id=1, source_target_pairs={{4,0},{8,4},{12,8},{16,12},{20,16},{24,20},{28,24},{5,1},{9,5},{13... | collective-permute-start | bytes 4616 | tf_op jit(solution)/shard_map/ppermute | solution.py:22
  6.4 7.6 %copy-start.6 = (s32[8,128]{1,0:T(8,128)S(1)}, s32[8,128]{1,0:T(8,128)}, u32[]{:S(2)}) copy-start(s32[8,128]{1,0:T(8,128)} %param.15) | copy-start | bytes 12292
  7.5 18.8 %collective-permute-start.4 = (f32[54,1,128]{2,1,0:T(1,128)S(1)}, f32[54,1,128]{2,1,0:T(1,128)S(1)}, u32[]{:S(2)}, u32[]{:S(2)}) collective-permute-start(f32[54,1,128]{2,1,0:T(1,128)S(1)} %get-tuple-element.15), channel_id=1, source_target_pairs={{0,4},{4,8},{8,12},{12,16},{16,20},{20,24},{24,28},{1,5},{5,9},{9,... | collective-permute-start | bytes 82952 | tf_op jit(solution)/shard_map/ppermute | solution.py:21
  12.0 14.3 %collective-permute-start.5 = (f32[54,1,128]{2,1,0:T(1,128)S(1)}, f32[54,1,128]{2,1,0:T(1,128)S(1)}, u32[]{:S(2)}, u32[]{:S(2)}) collective-permute-start(f32[54,1,128]{2,1,0:T(1,128)S(1)} %get-tuple-element.16), channel_id=1, source_target_pairs={{4,0},{8,4},{12,8},{16,12},{20,16},{24,20},{28,24},{5,1},{9,5},{13... | collective-permute-start | bytes 82952 | tf_op jit(solution)/shard_map/ppermute | solution.py:22
  15.1 1.0 copy-start.3
  15.1 1.0 copy-start.4
  16.2 10.1 %copy-start.1 = (f32[54,8,128]{2,1,0:T(8,128)S(1)}, f32[54,8,128]{2,1,0:T(8,128)}, u32[]{:S(2)}) copy-start(f32[54,8,128]{2,1,0:T(8,128)} %param.11) | copy-start | bytes 663556
  16.2 9.7 %collective-permute-start.2 = (f32[3,10,1]{2,1,0:T(8,128)S(1)}, f32[3,10,1]{2,1,0:T(8,128)S(1)}, u32[]{:S(2)}, u32[]{:S(2)}) collective-permute-start(f32[3,10,1]{2,1,0:T(8,128)S(1)} %get-tuple-element.20), channel_id=1, source_target_pairs={{0,1},{1,2},{2,3},{4,5},{5,6},{6,7},{8,9},{9,10},{10,11},{12,13},{... | collective-permute-start | bytes 368 | tf_op jit(solution)/shard_map/ppermute | solution.py:21
  17.7 8.3 %collective-permute-start.3 = (f32[3,10,1]{2,1,0:T(8,128)S(1)}, f32[3,10,1]{2,1,0:T(8,128)S(1)}, u32[]{:S(2)}, u32[]{:S(2)}) collective-permute-start(f32[3,10,1]{2,1,0:T(8,128)S(1)} %get-tuple-element.21), channel_id=1, source_target_pairs={{1,0},{2,1},{3,2},{5,4},{6,5},{7,6},{9,8},{10,9},{11,10},{13,12},{... | collective-permute-start | bytes 368 | tf_op jit(solution)/shard_map/ppermute | solution.py:22
  26.6 11.3 %collective-permute-start.6 = (f32[54,10,1]{2,1,0:T(8,128)S(1)}, f32[54,10,1]{2,1,0:T(8,128)S(1)}, u32[]{:S(2)}, u32[]{:S(2)}) collective-permute-start(f32[54,10,1]{2,1,0:T(8,128)S(1)} %get-tuple-element.10), channel_id=1, source_target_pairs={{1,0},{2,1},{3,2},{5,4},{6,5},{7,6},{9,8},{10,9},{11,10},{13,12},{... | collective-permute-start | bytes 6488 | tf_op jit(solution)/shard_map/ppermute | solution.py:22
  28.7 13.0 %collective-permute-start.7 = (f32[54,10,1]{2,1,0:T(8,128)S(1)}, f32[54,10,1]{2,1,0:T(8,128)S(1)}, u32[]{:S(2)}, u32[]{:S(2)}) collective-permute-start(f32[54,10,1]{2,1,0:T(8,128)S(1)} %get-tuple-element.9), channel_id=1, source_target_pairs={{0,1},{1,2},{2,3},{4,5},{5,6},{6,7},{8,9},{9,10},{10,11},{12,13},{... | collective-permute-start | bytes 6488 | tf_op jit(solution)/shard_map/ppermute | solution.py:21
  42.3 6.1 %collective-permute-start.8 = (f32[54,1,128]{2,1,0:T(1,128)S(1)}, f32[54,1,128]{2,1,0:T(1,128)S(1)}, u32[]{:S(2)}, u32[]{:S(2)}) collective-permute-start(f32[54,1,128]{2,1,0:T(1,128)S(1)} %get-tuple-element.13), channel_id=1, source_target_pairs={{0,4},{4,8},{8,12},{12,16},{16,20},{20,24},{24,28},{1,5},{5,9},{9,... | collective-permute-start | bytes 82952 | tf_op jit(solution)/shard_map/ppermute | solution.py:21
  45.8 6.1 %collective-permute-start.9 = (f32[54,1,128]{2,1,0:T(1,128)S(1)}, f32[54,1,128]{2,1,0:T(1,128)S(1)}, u32[]{:S(2)}, u32[]{:S(2)}) collective-permute-start(f32[54,1,128]{2,1,0:T(1,128)S(1)} %get-tuple-element.14), channel_id=1, source_target_pairs={{4,0},{8,4},{12,8},{16,12},{20,16},{24,20},{28,24},{5,1},{9,5},{13... | collective-permute-start | bytes 82952 | tf_op jit(solution)/shard_map/ppermute | solution.py:22
  52.2 11.4 %collective-permute-start.10 = (f32[54,10,1]{2,1,0:T(8,128)S(1)}, f32[54,10,1]{2,1,0:T(8,128)S(1)}, u32[]{:S(2)}, u32[]{:S(2)}) collective-permute-start(f32[54,10,1]{2,1,0:T(8,128)S(1)} %get-tuple-element.8), channel_id=1, source_target_pairs={{1,0},{2,1},{3,2},{5,4},{6,5},{7,6},{9,8},{10,9},{11,10},{13,12},{... | collective-permute-start | bytes 6488 | tf_op jit(solution)/shard_map/ppermute | solution.py:22
  54.3 13.4 %collective-permute-start.11 = (f32[54,10,1]{2,1,0:T(8,128)S(1)}, f32[54,10,1]{2,1,0:T(8,128)S(1)}, u32[]{:S(2)}, u32[]{:S(2)}) collective-permute-start(f32[54,10,1]{2,1,0:T(8,128)S(1)} %get-tuple-element.7), channel_id=1, source_target_pairs={{0,1},{1,2},{2,3},{4,5},{5,6},{6,7},{8,9},{9,10},{10,11},{12,13},{... | collective-permute-start | bytes 6488 | tf_op jit(solution)/shard_map/ppermute | solution.py:21
  68.2 5.3 %collective-permute-start.12 = (f32[54,1,128]{2,1,0:T(1,128)S(1)}, f32[54,1,128]{2,1,0:T(1,128)S(1)}, u32[]{:S(2)}, u32[]{:S(2)}) collective-permute-start(f32[54,1,128]{2,1,0:T(1,128)S(1)} %get-tuple-element.11), channel_id=1, source_target_pairs={{0,4},{4,8},{8,12},{12,16},{16,20},{20,24},{24,28},{1,5},{5,9},{9,... | collective-permute-start | bytes 82952 | tf_op jit(solution)/shard_map/ppermute | solution.py:21
  70.3 6.1 %collective-permute-start.13 = (f32[54,1,128]{2,1,0:T(1,128)S(1)}, f32[54,1,128]{2,1,0:T(1,128)S(1)}, u32[]{:S(2)}, u32[]{:S(2)}) collective-permute-start(f32[54,1,128]{2,1,0:T(1,128)S(1)} %get-tuple-element.12), channel_id=1, source_target_pairs={{4,0},{8,4},{12,8},{16,12},{20,16},{24,20},{28,24},{5,1},{9,5},{13... | collective-permute-start | bytes 82952 | tf_op jit(solution)/shard_map/ppermute | solution.py:22
  76.6 11.6 %collective-permute-start.14 = (f32[54,10,1]{2,1,0:T(8,128)S(1)}, f32[54,10,1]{2,1,0:T(8,128)S(1)}, u32[]{:S(2)}, u32[]{:S(2)}) collective-permute-start(f32[54,10,1]{2,1,0:T(8,128)S(1)} %get-tuple-element.6), channel_id=1, source_target_pairs={{1,0},{2,1},{3,2},{5,4},{6,5},{7,6},{9,8},{10,9},{11,10},{13,12},{... | collective-permute-start | bytes 6488 | tf_op jit(solution)/shard_map/ppermute | solution.py:22
  78.6 14.0 %collective-permute-start.15 = (f32[54,10,1]{2,1,0:T(8,128)S(1)}, f32[54,10,1]{2,1,0:T(8,128)S(1)}, u32[]{:S(2)}, u32[]{:S(2)}) collective-permute-start(f32[54,10,1]{2,1,0:T(8,128)S(1)} %get-tuple-element.5), channel_id=1, source_target_pairs={{0,1},{1,2},{2,3},{4,5},{5,6},{6,7},{8,9},{9,10},{10,11},{12,13},{... | collective-permute-start | bytes 6488 | tf_op jit(solution)/shard_map/ppermute | solution.py:21
  94.6 0.8 copy-start.8
  95.5 0.7 copy-start.2
  95.5 0.7 copy-start.5
  (3 other events, 2.1 us)
where the time goes:
time: 106 us; the launch traced here: 105 us
  waiting for transfers between devices  42.4 us (40%)
  starting transfers between devices  37.2 us (35%)
  local copies, waits for them, and re-layouts  11.8 us (11%)
  other arithmetic  8.24 us (8%)
  matrix products  4.9 us (5%)
    ppermute x8, waiting for transfers between devices, extended(): after = lax.ppermute(initial, axis, down)  30.1 us
    ppermute x8, starting transfers between devices, extended(): before = lax.ppermute(last, axis, up)  19.1 us
    ppermute x8, starting transfers between devices, extended(): after = lax.ppermute(initial, axis, down)  18.1 us
    ppermute x8, waiting for transfers between devices, extended(): before = lax.ppermute(last, axis, up)  12.3 us
    scatter x1, local copies, waits for them, and re-layouts, shards(): slot_cell = jnp.zeros((cell_capacity + 1,), jnp.int32).at[jnp.where(activ...  4.3 us
    dot_general x8, matrix products, network(): jnp.dot(hidden_level_matrix, hidden, preferred_element_type=jnp.float32)  3.28 us
    scatter-add x1, other arithmetic, shards(): increments = jnp.zeros((species_count, cell_total + 1), jnp.float32).at[:...  3.21 us
    unnamed x23, local copies, waits for them, and re-layouts  2.68 us
  transfers between devices with their start and end apart: 16, of which 8 were waited for; matrix products, arithmetic and copies ran while one was open for 9% of the time, Pallas kernels for 0%

commit v1 on v0

v1 whole, which is shorter than its diff:
```python
import functools

import jax
import jax.numpy as jnp
from jax import lax
from jax.experimental import pallas as pl
from jax.experimental.pallas import tpu as pltpu
from jax.sharding import PartitionSpec as P

SUBSTEPS = 8
TRANSPORT_STEPS = 3
CHEM_STEP = 0.0625
GROUP = 4
SLOT = 8
CHUNKS = 4
MESH_ID = pl.DeviceIdType.MESH
DIRECTIONS = tuple((dr, dc) for dr in (-1, 0, 1) for dc in (-1, 0, 1) if (dr, dc) != (0, 0))


def roll_lanes(x, shift):
    return pltpu.roll(x, shift % x.shape[-1], x.ndim - 1)


def roll_rows(x, shift):
    return pltpu.roll(x, shift % x.shape[-2], x.ndim - 2)


def around_rows(centre, outer, first, last):
    cu, hu = roll_rows(centre, -1), roll_rows(outer, -1)
    cd, hd = roll_rows(centre, 1), roll_rows(outer, 1)
    return (
        jnp.where(last, hu, cu),
        jnp.where(first, hd, cd),
        jnp.where(last, cu, hu),
        jnp.where(first, cd, hd),
    )


def coefficients(d, u, v, de, dw, dn, ds, ue, uw, vn, vs):
    de, dw, dn, ds = (0.5 * (d + x) for x in (de, dw, dn, ds))
    ue, uw, vn, vs = 0.5 * (u + ue), 0.5 * (u + uw), 0.5 * (v + vn), 0.5 * (v + vs)
    own = (
        1.0
        - (de + jnp.maximum(ue, 0.0))
        - (dw - jnp.minimum(uw, 0.0))
        - (dn + jnp.maximum(vn, 0.0))
        - (ds - jnp.minimum(vs, 0.0))
    )
    return (
        own,
        de - jnp.minimum(ue, 0.0),
        dw + jnp.maximum(uw, 0.0),
        dn - jnp.minimum(vn, 0.0),
        ds + jnp.maximum(vs, 0.0),
    )


def apply_step(w, own, east, west, north, south):
    return w[0] * own + w[1] * east + w[2] * west + w[3] * north + w[4] * south


def kernel(
    rows, cols, species,
    mix_hbm, diff_hbm, speed_hbm, heat_hbm, active_hbm, w1_hbm, w2_hbm, w3_hbm,
    b1_ref, b2_ref, b3_ref,
    out_ref,
    field, halo, side, corner, next_c, next_h, adv, heat_v, active_v, w1_v, w2_v, w3_v, w1_p, w3_p, b3_p,
    local_sem, send_sem, recv_sem,
):
    r, c = lax.axis_index("row"), lax.axis_index("col")
    padded = pl.cdiv(species, GROUP) * GROUP
    slots = padded // GROUP
    coef = padded
    packed = padded + GROUP

    loads = [
        pltpu.make_async_copy(mix_hbm, field.at[pl.ds(0, species)], local_sem.at[0]),
        pltpu.make_async_copy(diff_hbm, field.at[coef], local_sem.at[1]),
        pltpu.make_async_copy(speed_hbm, field.at[pl.ds(coef + 1, 2)], local_sem.at[2]),
        pltpu.make_async_copy(heat_hbm, heat_v, local_sem.at[3]),
        pltpu.make_async_copy(active_hbm, active_v, local_sem.at[4]),
        pltpu.make_async_copy(w1_hbm, w1_v, local_sem.at[5]),
        pltpu.make_async_copy(w2_hbm, w2_v, local_sem.at[6]),
        pltpu.make_async_copy(w3_hbm, w3_v, local_sem.at[7]),
    ]
    for load in loads:
        load.start()
    halo[...] = jnp.zeros_like(halo)
    side[...] = jnp.zeros_like(side)
    corner[...] = jnp.zeros_like(corner)

    def there(dr, dc):
        ok = jnp.bool_(True)
        if dr:
            ok = jnp.logical_and(ok, r + dr < rows if dr > 0 else r + dr >= 0)
        if dc:
            ok = jnp.logical_and(ok, c + dc < cols if dc > 0 else c + dc >= 0)
        return ok

    barrier = pltpu.get_barrier_semaphore()
    for dr, dc in DIRECTIONS:
        @pl.when(there(dr, dc))
        def _(dr=dr, dc=dc):
            pl.semaphore_signal(barrier, inc=1, device_id=(r + dr, c + dc), device_id_type=MESH_ID)

    for s in [*range(species, padded), coef + 3]:
        field[s] = jnp.zeros(field.shape[1:], jnp.float32)
    lane = lax.broadcasted_iota(jnp.int32, (8, 128), 1)
    row = lax.broadcasted_iota(jnp.int32, (8, 128), 0)
    first, last = row == 0, row == 7
    west_end, east_end = lane == 0, lane == 127
    in_slot = lane % SLOT
    slot = lane // SLOT
    for load in loads[:3]:
        load.wait()
    pack = jnp.zeros((GROUP, 8, 128), jnp.float32)
    for k in range(slots + 1):
        pack = jnp.where(slot == k, roll_lanes(field[pl.ds(GROUP * k, GROUP)], SLOT * k + 3), pack)
    field[pl.ds(packed, GROUP)] = pack

    one = lambda ok: jnp.where(ok, 1, 0)
    row_sides, col_sides = one(r > 0) + one(r < rows - 1), one(c > 0) + one(c < cols - 1)
    pl.semaphore_wait(barrier, (1 + row_sides) * (1 + col_sides) - 1)

    def message(index):
        dr, dc = DIRECTIONS[index]
        strip = {1: pl.ds(5, 3), -1: pl.ds(0, 3), 0: pl.ds(0, 8)}[dr]
        if dc == 0:
            src, dst = field.at[:, strip, :], halo.at[:, strip, :]
        else:
            target = side if dr == 0 else corner
            src = field.at[pl.ds(packed, GROUP), strip, :]
            dst = target.at[pl.ds(0 if dc > 0 else GROUP, GROUP), strip, :]
        return pltpu.make_async_remote_copy(
            src_ref=src, dst_ref=dst, send_sem=send_sem.at[index], recv_sem=recv_sem.at[index],
            device_id=(r + dr, c + dc), device_id_type=MESH_ID,
        )

    for index, (dr, dc) in enumerate(DIRECTIONS):
        @pl.when(there(dr, dc))
        def _(index=index):
            message(index).start()

    for load in loads[3:]:
        load.wait()
    w1_p[...] = jnp.zeros_like(w1_p)
    w1_p[pl.ds(0, species + 1), :] = w1_v[...]
    first_matrix = jnp.transpose(w1_p[...].astype(jnp.float32)).astype(jnp.bfloat16)
    w3_p[...] = jnp.zeros_like(w3_p)
    w3_p[pl.ds(0, species), :] = w3_v[...]
    hidden = w1_v.shape[1]
    bias1 = jnp.transpose(jnp.broadcast_to(b1_ref[...], (128, hidden)))
    bias2 = jnp.transpose(jnp.broadcast_to(b2_ref[...], (128, hidden)))
    b3_p[...] = jnp.zeros_like(b3_p)
    b3_p[:, pl.ds(0, species)] = b3_ref[...]
    bias3 = jnp.transpose(jnp.broadcast_to(b3_p[...], (128, 128)))[:64]

    for index, (dr, dc) in enumerate(DIRECTIONS):
        @pl.when(there(-dr, -dc))
        def _(index=index):
            message(index).wait_recv()

    own_c, own_h = field[pl.ds(packed, GROUP)], halo[pl.ds(packed, GROUP)]
    lower = in_slot < 3
    faces = [
        (jnp.where(lower, side[:GROUP], own_c), jnp.where(lower, corner[:GROUP], own_h)),
        (jnp.where(lower, own_c, side[GROUP:]), jnp.where(lower, own_h, corner[GROUP:])),
    ]
    in_outer = jnp.where(row < 4, jnp.where(r < rows - 1, 1.0, 0.0), jnp.where(r > 0, 1.0, 0.0))
    in_left = jnp.where(lower, jnp.where(c > 0, 1.0, 0.0), 1.0)
    in_right = jnp.where(lower, 1.0, jnp.where(c < cols - 1, 1.0, 0.0))

    def joined(left, right):
        return jnp.where(in_slot == 7, roll_lanes(right, -4), roll_lanes(left, -2))

    def around_lanes(x, join, k):
        moved = roll_lanes(join, -SLOT * k)
        return jnp.where(east_end, moved, roll_lanes(x, -1)), jnp.where(west_end, moved, roll_lanes(x, 1))

    def replicate(x):
        x = jnp.where(slot == slots, x, 0.0)
        for step in (8, 16, 32, 64):
            x = x + roll_lanes(x, step)
        return x

    def weights(dc_, uc, vc, dh, uh, vh, lanes_c, lanes_h, mask_c, mask_h):
        dnc, dsc, dnh, dsh = around_rows(dc_, dh, first, last)
        vnc, vsc, vnh, vsh = around_rows(vc, vh, first, last)
        (dec, dwc), (uec, uwc) = lanes_c
        (deh, dwh), (ueh, uwh) = lanes_h
        wc = coefficients(dc_, uc, vc, dec, dwc, dnc, dsc, uec, uwc, vnc, vsc)
        wh = coefficients(dh, uh, vh, deh, dwh, dnh, dsh, ueh, uwh, vnh, vsh)
        if mask_c is not None:
            wc = tuple(w * mask_c for w in wc)
        return wc, tuple(w * mask_h for w in wh)

    face_w = []
    for (fc, fh), mask in zip(faces, (in_left, in_right)):
        dc_, uc, vc = (replicate(fc[i]) for i in range(3))
        dh, uh, vh = (replicate(fh[i]) for i in range(3))
        pair = lambda x: (roll_lanes(x, -1), roll_lanes(x, 1))
        face_w.append(weights(dc_, uc, vc, dh, uh, vh, (pair(dc_), pair(uc)), (pair(dh), pair(uh)), mask, mask * in_outer))
    join_c, join_h = joined(faces[0][0], faces[1][0]), joined(faces[0][1], faces[1][1])
    tile_c, tile_h = field[pl.ds(coef, 3)], halo[pl.ds(coef, 3)]
    lanes_c = tuple(around_lanes(tile_c[i], join_c[i], slots) for i in range(2))
    lanes_h = tuple(around_lanes(tile_h[i], join_h[i], slots) for i in range(2))
    wc, wh = weights(*(tile_c[i] for i in range(3)), *(tile_h[i] for i in range(3)), lanes_c, lanes_h, None, in_outer)

    for step in range(TRANSPORT_STEPS):
        final = step == TRANSPORT_STEPS - 1
        for k in range(slots):
            here = pl.ds(GROUP * k, GROUP)
            xc, xh = (field[here], halo[here]) if step == 0 else (next_c[here], next_h[here])
            nc, sc, nh, sh = around_rows(xc, xh, first, last)
            ec, wcc = around_lanes(xc, join_c, k)
            new = apply_step(wc, xc, ec, wcc, nc, sc)
            if final:
                adv[here] = new
            else:
                eh, whh = around_lanes(xh, join_h, k)
                next_c[here] = new
                next_h[here] = apply_step(wh, xh, eh, whh, nh, sh)
        if not final:
            moved = []
            for (fc, fh), (fwc, fwh) in zip(faces, face_w):
                nc, sc, nh, sh = around_rows(fc, fh, first, last)
                moved.append((
                    apply_step(fwc, fc, roll_lanes(fc, -1), roll_lanes(fc, 1), nc, sc),
                    apply_step(fwh, fh, roll_lanes(fh, -1), roll_lanes(fh, 1), nh, sh),
                ))
            faces = moved
            join_c, join_h = joined(faces[0][0], faces[1][0]), joined(faces[0][1], faces[1][1])

    adv[species] = heat_v[...]
    for s in range(species + 1, adv.shape[0]):
        adv[s] = jnp.zeros(adv.shape[1:], jnp.float32)
    per = 8 // CHUNKS
    bases = [
        jnp.concatenate([adv[:, per * i + j, :] for j in range(per)], axis=1) for i in range(CHUNKS)
    ]
    wide = lambda b: jnp.concatenate([b] * per, axis=1)
    wide1, wide2, wide3 = wide(bias1), wide(bias2), wide(bias3)

    def substep(_, totals):
        new = []
        for base, total in zip(bases, totals):
            x = (base + CHEM_STEP * total).astype(jnp.bfloat16)
            h = jnp.dot(first_matrix, x, preferred_element_type=jnp.float32)
            h = jnp.tanh(h + wide1).astype(jnp.bfloat16)
            h = jnp.dot(w2_v[...], h, preferred_element_type=jnp.float32)
            h = jnp.tanh(h + wide2).astype(jnp.bfloat16)
            new.append(total + (jnp.dot(w3_p[...], h, preferred_element_type=jnp.float32) + wide3))
        return tuple(new)

    totals = lax.fori_loop(0, SUBSTEPS, substep, tuple(jnp.zeros_like(b) for b in bases))
    scale = CHEM_STEP * active_v[...].astype(jnp.float32)
    for i in range(CHUNKS):
        for j in range(per):
            q = per * i + j
            total = totals[i][:, 128 * j : 128 * (j + 1)]
            out_ref[:, q, :] = (adv[:, q, :] + scale[q : q + 1] * total)[:species]

    for index, (dr, dc) in enumerate(DIRECTIONS):
        @pl.when(there(dr, dc))
        def _(index=index):
            message(index).wait_send()


def shards(rows, cols, mix, diff, speed, heat, active, w1, b1, w2, b2, w3, b3):
    species, height, width = mix.shape
    padded = pl.cdiv(species, GROUP) * GROUP
    fields = padded + 2 * GROUP
    hidden, features = w1.shape
    vm = pltpu.VMEM
    f32, bf16 = jnp.float32, jnp.bfloat16
    return pl.pallas_call(
        functools.partial(kernel, rows, cols, species),
        out_shape=jax.ShapeDtypeStruct(mix.shape, mix.dtype),
        in_specs=[pl.BlockSpec(memory_space=pl.ANY)] * 8 + [pl.BlockSpec(memory_space=vm)] * 3,
        out_specs=pl.BlockSpec(memory_space=vm),
        scratch_shapes=[
            vm((fields, height, width), f32),
            vm((fields, height, width), f32),
            vm((2 * GROUP, height, width), f32),
            vm((2 * GROUP, height, width), f32),
            vm((padded, height, width), f32),
            vm((padded, height, width), f32),
            vm((64, height, width), f32),
            vm((height, width), f32),
            vm((height, width), jnp.int32),
            vm((features, hidden), bf16),
            vm(w2.shape, bf16),
            vm(w3.shape, bf16),
            vm((64, hidden), bf16),
            vm((64, hidden), bf16),
            vm((1, 128), f32),
            pltpu.SemaphoreType.DMA((8,)),
            pltpu.SemaphoreType.DMA((8,)),
            pltpu.SemaphoreType.DMA((8,)),
        ],
        compiler_params=pltpu.CompilerParams(collective_id=0, has_side_effects=True),
    )(mix, diff, speed, heat, active, w1.T, w2, w3,
      b1[None], b2[None], b3[None])


def solution(mesh):
    tile = P(None, "row", "col")
    plane = P("row", "col")
    return jax.shard_map(
        functools.partial(shards, mesh.shape["row"], mesh.shape["col"]),
        mesh=mesh,
        in_specs=(tile, plane, tile, plane, plane, P(), P(), P(), P(), P(), P()),
        out_specs=tile,
        check_vma=False,
    )
```

time: 106 us -> 25.1 us (0.24)
  the two profiles are of different devices: /device:TPU:27 before, /device:TPU:1 now
where the time goes in v1:
time: 25.1 us; the launch traced here: 25 us
  Pallas kernels  23.3 us (93%)
  local copies, waits for them, and re-layouts  1.64 us (7%)
    pallas_call x1, Pallas kernels, shards(): pl.pallas_call(functools.partial(kernel, rows, cols, species), out_shape=...  23.3 us
    unnamed x1, local copies, waits for them, and re-layouts  1.64 us

profile of v1, /device:TPU:1, one launch (start us, length us, event | category | flops | bytes accessed | tf_op | source)
XLA Modules:
  0.0 25.0 jit_solution(7822196026405389305)
XLA Ops:
  0.0 23.3 %shard_map.109 = f32[54,8,128]{2,1,0:T(8,128)} custom-call(f32[54,8,128]{2,1,0:T(8,128)} %mix_hbm.1, f32[8,128]{1,0:T(8,128)} %diff_hbm.1, f32[2,8,128]{2,1,0:T(8,128)} %speed_hbm.1, f32[8,128]{1,0:T(8,128)} %heat_hbm.1, s32[8,128]{1,0:T(8,128)} %active_hbm.1, bf16[55,256]{1,0:T(8,128)(2,1)} %bitcast.4, bf16[256,256]{1,0:T(8,128)(2,1)} %w2_hbm.1, ...), custom_call_target="tpu_custom_call" | custom-call | tf_op jit(solution)/shard_map/pallas_call | solution.py:276
  23.3 1.6 %copy.13 = f32[54,8,128]{2,1,0:T(8,128)} copy(f32[54,8,128]{2,1,0:T(8,128)} %shard_map.109) | data formatting | bytes 442368

commit v2 on v1

--- a/solution.py
+++ b/solution.py
@@ -12,7 +12,9 @@
 CHEM_STEP = 0.0625
 GROUP = 4
 SLOT = 8
-CHUNKS = 4
+CHUNKS = 2
+WIDTH = 64
+UNROLL = 1
 MESH_ID = pl.DeviceIdType.MESH
 DIRECTIONS = tuple((dr, dc) for dr in (-1, 0, 1) for dc in (-1, 0, 1) if (dr, dc) != (0, 0))
 
@@ -64,7 +66,7 @@
     mix_hbm, diff_hbm, speed_hbm, heat_hbm, active_hbm, w1_hbm, w2_hbm, w3_hbm,
     b1_ref, b2_ref, b3_ref,
     out_ref,
-    field, halo, side, corner, next_c, next_h, adv, heat_v, active_v, w1_v, w2_v, w3_v, w1_p, w3_p, b3_p,
+    field, halo, side, corner, next_c, next_h, adv, heat_v, active_v, w1_v, w2_v, w3_v, w1_p, w2_p, w3_s, w3_p, b3_p, chosen, spread,
     local_sem, send_sem, recv_sem,
 ):
     r, c = lax.axis_index("row"), lax.axis_index("col")
@@ -145,15 +147,27 @@
         load.wait()
     w1_p[...] = jnp.zeros_like(w1_p)
     w1_p[pl.ds(0, species + 1), :] = w1_v[...]
-    first_matrix = jnp.transpose(w1_p[...].astype(jnp.float32)).astype(jnp.bfloat16)
-    w3_p[...] = jnp.zeros_like(w3_p)
-    w3_p[pl.ds(0, species), :] = w3_v[...]
-    hidden = w1_v.shape[1]
-    bias1 = jnp.transpose(jnp.broadcast_to(b1_ref[...], (128, hidden)))
-    bias2 = jnp.transpose(jnp.broadcast_to(b2_ref[...], (128, hidden)))
+    w2_p[...] = jnp.transpose(w2_v[...].astype(jnp.float32)).astype(jnp.bfloat16)
+    w3_s[...] = jnp.zeros_like(w3_s)
+    w3_s[pl.ds(0, species), :] = w3_v[...]
+    w3_p[...] = jnp.transpose(w3_s[...].astype(jnp.float32)).astype(jnp.bfloat16)
     b3_p[...] = jnp.zeros_like(b3_p)
     b3_p[:, pl.ds(0, species)] = b3_ref[...]
-    bias3 = jnp.transpose(jnp.broadcast_to(b3_p[...], (128, 128)))[:64]
+
+    capacity = chosen.shape[0]
+    flags = jnp.where(active_v[...] == 1, 1.0, 0.0)
+    upto = lax.broadcasted_iota(jnp.int32, (128, 128), 0) <= lax.broadcasted_iota(jnp.int32, (128, 128), 1)
+    upto = jnp.where(upto, 1.0, 0.0).astype(jnp.bfloat16)
+    within = jnp.dot(flags.astype(jnp.bfloat16), upto, preferred_element_type=jnp.float32)
+    offset = jnp.dot(flags.astype(jnp.bfloat16), jnp.ones((128, 128), jnp.bfloat16), preferred_element_type=jnp.float32)
+    offset = jnp.where(row >= 1, roll_rows(offset, 1), 0.0)
+    for shift in (1, 2, 4):
+        offset = offset + jnp.where(row >= shift, roll_rows(offset, shift), 0.0)
+    place = jnp.where(flags > 0.0, within + offset - 1.0, -1.0)
+    index = lax.broadcasted_iota(jnp.int32, (capacity, 128), 0).astype(jnp.float32)
+    for q in range(8):
+        hit = index == place[q : q + 1]
+        chosen[:, 128 * q : 128 * (q + 1)] = jnp.where(hit, 1.0, 0.0).astype(jnp.bfloat16)
 
     for index, (dr, dc) in enumerate(DIRECTIONS):
         @pl.when(there(-dr, -dc))
@@ -215,7 +229,7 @@
             ec, wcc = around_lanes(xc, join_c, k)
             new = apply_step(wc, xc, ec, wcc, nc, sc)
             if final:
-                adv[here] = new
+                adv[pl.ds(8 * GROUP * k, 8 * GROUP), :] = new.reshape(8 * GROUP, 128)
             else:
                 eh, whh = around_lanes(xh, join_h, k)
                 next_c[here] = new
@@ -231,34 +245,48 @@
             faces = moved
             join_c, join_h = joined(faces[0][0], faces[1][0]), joined(faces[0][1], faces[1][1])
 
-    adv[species] = heat_v[...]
-    for s in range(species + 1, adv.shape[0]):
-        adv[s] = jnp.zeros(adv.shape[1:], jnp.float32)
-    per = 8 // CHUNKS
-    bases = [
-        jnp.concatenate([adv[:, per * i + j, :] for j in range(per)], axis=1) for i in range(CHUNKS)
-    ]
-    wide = lambda b: jnp.concatenate([b] * per, axis=1)
-    wide1, wide2, wide3 = wide(bias1), wide(bias2), wide(bias3)
+    adv[pl.ds(8 * species, 8), :] = heat_v[...]
+    adv[pl.ds(8 * (species + 1), 8 * (WIDTH - species - 1)), :] = jnp.zeros((8 * (WIDTH - species - 1), 128), jnp.float32)
+    gathered = None
+    for p in range(4):
+        x = jnp.concatenate([adv[pl.ds(2 * p + j, WIDTH, stride=8), :] for j in range(2)], axis=1)
+        terms = []
+        for _ in range(3):
+            terms.append(x.astype(jnp.bfloat16))
+            x = x - terms[-1].astype(jnp.float32)
+        part = lax.dot_general(
+            chosen[:, 256 * p : 256 * (p + 1)], jnp.concatenate(terms, axis=0),
+            (((1,), (1,)), ((), ())), preferred_element_type=jnp.float32,
+        )
+        gathered = part if gathered is None else gathered + part
+    low = jnp.concatenate([gathered[:, 128:], jnp.zeros((capacity, WIDTH), jnp.float32)], axis=1)
+    state = gathered[:, :128] + roll_lanes(gathered[:, :128], WIDTH) + low
+    chunk = capacity // CHUNKS
+    bases = [state[chunk * i : chunk * (i + 1)] for i in range(CHUNKS)]
+    bias1, bias2, bias3 = b1_ref[...], b2_ref[...], b3_p[...]
 
     def substep(_, totals):
-        new = []
-        for base, total in zip(bases, totals):
-            x = (base + CHEM_STEP * total).astype(jnp.bfloat16)
-            h = jnp.dot(first_matrix, x, preferred_element_type=jnp.float32)
-            h = jnp.tanh(h + wide1).astype(jnp.bfloat16)
-            h = jnp.dot(w2_v[...], h, preferred_element_type=jnp.float32)
-            h = jnp.tanh(h + wide2).astype(jnp.bfloat16)
-            new.append(total + (jnp.dot(w3_p[...], h, preferred_element_type=jnp.float32) + wide3))
-        return tuple(new)
-
-    totals = lax.fori_loop(0, SUBSTEPS, substep, tuple(jnp.zeros_like(b) for b in bases))
-    scale = CHEM_STEP * active_v[...].astype(jnp.float32)
-    for i in range(CHUNKS):
-        for j in range(per):
-            q = per * i + j
-            total = totals[i][:, 128 * j : 128 * (j + 1)]
-            out_ref[:, q, :] = (adv[:, q, :] + scale[q : q + 1] * total)[:species]
+        hs = [(base + CHEM_STEP * total).astype(jnp.bfloat16) for base, total in zip(bases, totals)]
+        hs = [jnp.dot(x, w1_p[...], preferred_element_type=jnp.float32) for x in hs]
+        hs = [jnp.tanh(h + bias1).astype(jnp.bfloat16) for h in hs]
+        hs = [jnp.dot(h, w2_p[...], preferred_element_type=jnp.float32) for h in hs]
+        hs = [jnp.tanh(h + bias2).astype(jnp.bfloat16) for h in hs]
+        hs = [jnp.dot(h, w3_p[...], preferred_element_type=jnp.float32) for h in hs]
+        return tuple(total + (h + bias3) for total, h in zip(totals, hs))
+
+    totals = tuple(jnp.zeros_like(b) for b in bases)
+    totals = lax.fori_loop(0, SUBSTEPS, substep, totals, unroll=UNROLL)
+    total = CHEM_STEP * jnp.transpose(jnp.concatenate(totals, axis=0))[:WIDTH]
+    high = total.astype(jnp.bfloat16)
+    low = (total - high.astype(jnp.float32)).astype(jnp.bfloat16)
+    both = jnp.concatenate([high, low], axis=0)
+    for p in range(4):
+        part = jnp.dot(both, chosen[:, 256 * p : 256 * (p + 1)], preferred_element_type=jnp.float32)
+        part = part[:WIDTH] + part[WIDTH:]
+        for j in range(2):
+            spread[pl.ds(WIDTH * (2 * p + j), WIDTH), :] = part[:, 128 * j : 128 * (j + 1)]
+    for s in range(species):
+        out_ref[s] = adv[pl.ds(8 * s, 8), :] + spread[pl.ds(s, 8, stride=WIDTH), :]
 
     for index, (dr, dc) in enumerate(DIRECTIONS):
         @pl.when(there(dr, dc))
@@ -276,7 +304,7 @@
     return pl.pallas_call(
         functools.partial(kernel, rows, cols, species),
         out_shape=jax.ShapeDtypeStruct(mix.shape, mix.dtype),
-        in_specs=[pl.BlockSpec(memory_space=pl.ANY)] * 8 + [pl.BlockSpec(memory_space=vm)] * 3,
+        in_specs=[pl.BlockSpec(memory_space=pltpu.HBM)] * 8 + [pl.BlockSpec(memory_space=vm)] * 3,
         out_specs=pl.BlockSpec(memory_space=vm),
         scratch_shapes=[
             vm((fields, height, width), f32),
@@ -285,20 +313,24 @@
             vm((2 * GROUP, height, width), f32),
             vm((padded, height, width), f32),
             vm((padded, height, width), f32),
-            vm((64, height, width), f32),
+            vm((WIDTH * height, width), f32),
             vm((height, width), f32),
             vm((height, width), jnp.int32),
             vm((features, hidden), bf16),
             vm(w2.shape, bf16),
             vm(w3.shape, bf16),
-            vm((64, hidden), bf16),
-            vm((64, hidden), bf16),
+            vm((128, hidden), bf16),
+            vm((hidden, hidden), bf16),
+            vm((128, hidden), bf16),
+            vm((hidden, 128), bf16),
             vm((1, 128), f32),
+            vm((3 * (height * width // 8), height * width), bf16),
+            vm((WIDTH * height, width), f32),
             pltpu.SemaphoreType.DMA((8,)),
             pltpu.SemaphoreType.DMA((8,)),
             pltpu.SemaphoreType.DMA((8,)),
         ],
-        compiler_params=pltpu.CompilerParams(collective_id=0, has_side_effects=True),
+        compiler_params=pltpu.CompilerParams(collective_id=0, has_side_effects=True, vmem_limit_bytes=16 << 20),
     )(mix, diff, speed, heat, active, w1.T, w2, w3,
       b1[None], b2[None], b3[None])
 

time: 25.1 us -> 21.5 us (0.86); the launches traced: 25 us -> 21 us
  Pallas kernels: 23.3 us -> 14.2 us
  local copies, waits for them, and re-layouts: 1.64 us -> 6.79 us
    pallas_call x1, Pallas kernels: 23.3 us -> 14.2 us  [shards(): pl.pallas_call(functools.partial(kernel, rows, cols, species), out_shape=...]
    unnamed x1 -> x23, local copies, waits for them, and re-layouts: 1.64 us -> 6.79 us
where the time goes in v2:
time: 21.5 us; the launch traced here: 21 us
  Pallas kernels  14.2 us (66%)
  local copies, waits for them, and re-layouts  6.79 us (32%)
    pallas_call x1, Pallas kernels, shards(): pl.pallas_call(functools.partial(kernel, rows, cols, species), out_shape=...  14.2 us
    unnamed x23, local copies, waits for them, and re-layouts  6.79 us

profile of v2, /device:TPU:1, one launch (start us, length us, event | category | flops | bytes accessed | tf_op | source)
XLA Modules:
  0.0 21.0 jit_solution(15930850844811496702)
XLA Ops:
  0.0 0.0 copy-start.5
  0.0 0.0 copy-start.9
  0.0 0.0 copy-start.8
  0.0 0.0 copy-start.10
  0.0 0.7 %copy-done.5 = f32[8,128]{1,0:T(8,128)S(1)} copy-done((f32[8,128]{1,0:T(8,128)S(1)}, f32[8,128]{1,0:T(8,128)}, u32[]{:S(2)}) %copy-start.5) | copy-done | bytes 4120
  0.7 0.0 copy-done.9
  0.7 0.0 copy-done.8
  0.7 0.0 copy-done.10
  0.7 0.0 copy-start
  0.7 0.9 %copy-done = f32[54,8,128]{2,1,0:T(8,128)S(1)} copy-done((f32[54,8,128]{2,1,0:T(8,128)S(1)}, f32[54,8,128]{2,1,0:T(8,128)}, u32[]{:S(2)}) %copy-start) | copy-done | bytes 221208
  1.7 0.0 copy-start.1
  1.7 0.9 %copy-done.1 = bf16[256,256]{1,0:T(8,128)(2,1)S(1)} copy-done((bf16[256,256]{1,0:T(8,128)(2,1)S(1)}, bf16[256,256]{1,0:T(8,128)(2,1)}, u32[]{:S(2)}) %copy-start.1) | copy-done | bytes 131096
  2.6 0.0 copy-start.2
  2.6 0.7 %copy-done.2 = bf16[256,55]{0,1:T(8,128)(2,1)S(1)} copy-done((bf16[256,55]{0,1:T(8,128)(2,1)S(1)}, bf16[256,55]{0,1:T(8,128)(2,1)}, u32[]{:S(2)}) %copy-start.2) | copy-done | bytes 28184
  3.3 0.0 copy-start.3
  3.3 0.7 %copy-done.3 = bf16[54,256]{1,0:T(8,128)(2,1)S(1)} copy-done((bf16[54,256]{1,0:T(8,128)(2,1)S(1)}, bf16[54,256]{1,0:T(8,128)(2,1)}, u32[]{:S(2)}) %copy-start.3) | copy-done | bytes 27672
  4.1 0.0 copy-start.4
  4.1 0.7 %copy-done.4 = f32[2,8,128]{2,1,0:T(8,128)S(1)} copy-done((f32[2,8,128]{2,1,0:T(8,128)S(1)}, f32[2,8,128]{2,1,0:T(8,128)}, u32[]{:S(2)}) %copy-start.4) | copy-done | bytes 8216
  4.8 0.0 copy-start.6
  4.8 0.7 %copy-done.6 = f32[8,128]{1,0:T(8,128)S(1)} copy-done((f32[8,128]{1,0:T(8,128)S(1)}, f32[8,128]{1,0:T(8,128)}, u32[]{:S(2)}) %copy-start.6) | copy-done | bytes 4120
  5.4 0.0 copy-start.7
  5.4 0.7 %copy-done.7 = s32[8,128]{1,0:T(8,128)S(1)} copy-done((s32[8,128]{1,0:T(8,128)S(1)}, s32[8,128]{1,0:T(8,128)}, u32[]{:S(2)}) %copy-start.7) | copy-done | bytes 4120
  6.1 14.2 %shard_map.109 = f32[54,8,128]{2,1,0:T(8,128)S(1)} custom-call(f32[54,8,128]{2,1,0:T(8,128)S(1)} %copy-done, f32[8,128]{1,0:T(8,128)S(1)} %copy-done.5, f32[2,8,128]{2,1,0:T(8,128)S(1)} %copy-done.4, f32[8,128]{1,0:T(8,128)S(1)} %copy-done.6, s32[8,128]{1,0:T(8,128)S(1)} %copy-done.7, bf16[55,256]{1,0:T(8,128)(2,1)S(1)} %bitcast.4, ...), custom_call_target="tpu_custom_call" | custom-call | tf_op jit(solution)/shard_map/pallas_call | solution.py:304
  20.4 0.7 %copy.13 = f32[54,8,128]{2,1,0:T(8,128)} copy(f32[54,8,128]{2,1,0:T(8,128)S(1)} %shard_map.109) | data formatting | bytes 442368
Async XLA Ops:
  0.0 0.7 %copy-start.5 = (f32[8,128]{1,0:T(8,128)S(1)}, f32[8,128]{1,0:T(8,128)}, u32[]{:S(2)}) copy-start(f32[8,128]{1,0:T(8,128)} %diff_hbm.1) | copy-start | bytes 12292
  0.0 0.7 %copy-start.9 = (f32[256]{0:T(256)S(1)}, f32[256]{0:T(256)}, u32[]{:S(2)}) copy-start(f32[256]{0:T(256)} %param.19) | copy-start | bytes 3076
  0.0 0.7 %copy-start.8 = (f32[256]{0:T(256)S(1)}, f32[256]{0:T(256)}, u32[]{:S(2)}) copy-start(f32[256]{0:T(256)} %param.17) | copy-start | bytes 3076
  0.0 0.7 %copy-start.10 = (f32[54]{0:T(128)S(1)}, f32[54]{0:T(128)}, u32[]{:S(2)}) copy-start(f32[54]{0:T(128)} %param.21) | copy-start | bytes 652
  0.7 0.9 %copy-start = (f32[54,8,128]{2,1,0:T(8,128)S(1)}, f32[54,8,128]{2,1,0:T(8,128)}, u32[]{:S(2)}) copy-start(f32[54,8,128]{2,1,0:T(8,128)} %mix_hbm.1) | copy-start | bytes 663556
  1.7 0.9 %copy-start.1 = (bf16[256,256]{1,0:T(8,128)(2,1)S(1)}, bf16[256,256]{1,0:T(8,128)(2,1)}, u32[]{:S(2)}) copy-start(bf16[256,256]{1,0:T(8,128)(2,1)} %w2_hbm.1) | copy-start | bytes 393220
  2.6 0.7 %copy-start.2 = (bf16[256,55]{0,1:T(8,128)(2,1)S(1)}, bf16[256,55]{0,1:T(8,128)(2,1)}, u32[]{:S(2)}) copy-start(bf16[256,55]{0,1:T(8,128)(2,1)} %param.16) | copy-start | bytes 84484
  3.3 0.7 %copy-start.3 = (bf16[54,256]{1,0:T(8,128)(2,1)S(1)}, bf16[54,256]{1,0:T(8,128)(2,1)}, u32[]{:S(2)}) copy-start(bf16[54,256]{1,0:T(8,128)(2,1)} %w3_hbm.1) | copy-start | bytes 82948
  4.1 0.7 %copy-start.4 = (f32[2,8,128]{2,1,0:T(8,128)S(1)}, f32[2,8,128]{2,1,0:T(8,128)}, u32[]{:S(2)}) copy-start(f32[2,8,128]{2,1,0:T(8,128)} %speed_hbm.1) | copy-start | bytes 24580
  4.8 0.7 %copy-start.6 = (f32[8,128]{1,0:T(8,128)S(1)}, f32[8,128]{1,0:T(8,128)}, u32[]{:S(2)}) copy-start(f32[8,128]{1,0:T(8,128)} %heat_hbm.1) | copy-start | bytes 12292
  5.4 0.7 %copy-start.7 = (s32[8,128]{1,0:T(8,128)S(1)}, s32[8,128]{1,0:T(8,128)}, u32[]{:S(2)}) copy-start(s32[8,128]{1,0:T(8,128)} %active_hbm.1) | copy-start | bytes 12292

commit v3 on v2

--- a/solution.py
+++ b/solution.py
@@ -64,8 +64,9 @@
 def kernel(
     rows, cols, species,
     mix_hbm, diff_hbm, speed_hbm, heat_hbm, active_hbm, w1_hbm, w2_hbm, w3_hbm,
+    b1_hbm, b2_hbm, b3_hbm,
+    out_ref,
     b1_ref, b2_ref, b3_ref,
-    out_ref,
     field, halo, side, corner, next_c, next_h, adv, heat_v, active_v, w1_v, w2_v, w3_v, w1_p, w2_p, w3_s, w3_p, b3_p, chosen, spread,
     local_sem, send_sem, recv_sem,
 ):
@@ -84,6 +85,9 @@
         pltpu.make_async_copy(w1_hbm, w1_v, local_sem.at[5]),
         pltpu.make_async_copy(w2_hbm, w2_v, local_sem.at[6]),
         pltpu.make_async_copy(w3_hbm, w3_v, local_sem.at[7]),
+        pltpu.make_async_copy(b1_hbm, b1_ref, local_sem.at[8]),
+        pltpu.make_async_copy(b2_hbm, b2_ref, local_sem.at[9]),
+        pltpu.make_async_copy(b3_hbm, b3_ref, local_sem.at[10]),
     ]
     for load in loads:
         load.start()
@@ -301,12 +305,16 @@
     hidden, features = w1.shape
     vm = pltpu.VMEM
     f32, bf16 = jnp.float32, jnp.bfloat16
+    held = lambda x: pltpu.with_memory_space_constraint(x, pltpu.HBM)
     return pl.pallas_call(
         functools.partial(kernel, rows, cols, species),
         out_shape=jax.ShapeDtypeStruct(mix.shape, mix.dtype),
-        in_specs=[pl.BlockSpec(memory_space=pltpu.HBM)] * 8 + [pl.BlockSpec(memory_space=vm)] * 3,
+        in_specs=[pl.BlockSpec(memory_space=pltpu.HBM)] * 11,
         out_specs=pl.BlockSpec(memory_space=vm),
         scratch_shapes=[
+            vm((1, hidden), f32),
+            vm((1, hidden), f32),
+            vm((1, species), f32),
             vm((fields, height, width), f32),
             vm((fields, height, width), f32),
             vm((2 * GROUP, height, width), f32),
@@ -326,13 +334,12 @@
             vm((1, 128), f32),
             vm((3 * (height * width // 8), height * width), bf16),
             vm((WIDTH * height, width), f32),
-            pltpu.SemaphoreType.DMA((8,)),
+            pltpu.SemaphoreType.DMA((11,)),
             pltpu.SemaphoreType.DMA((8,)),
             pltpu.SemaphoreType.DMA((8,)),
         ],
         compiler_params=pltpu.CompilerParams(collective_id=0, has_side_effects=True, vmem_limit_bytes=16 << 20),
-    )(mix, diff, speed, heat, active, w1.T, w2, w3,
-      b1[None], b2[None], b3[None])
+    )(*(held(x) for x in (mix, diff, speed, heat, active, w1.T, w2, w3, b1[None], b2[None], b3[None])))
 
 
 def solution(mesh):

time: 21.5 us -> 14.6 us (0.68); the launches traced: 21 us -> 14.4 us
  local copies, waits for them, and re-layouts: 6.79 us -> 0.69 us
  Pallas kernels: 14.2 us -> 13.7 us
    unnamed x23 -> x1, local copies, waits for them, and re-layouts: 6.79 us -> 0.69 us
    pallas_call x1, Pallas kernels: 14.2 us -> 13.7 us  [shards(): pl.pallas_call(functools.partial(kernel, rows, cols, species), out_shape=...]
where the time goes in v3:
time: 14.6 us; the launch traced here: 14.4 us
  Pallas kernels  13.7 us (94%)
  local copies, waits for them, and re-layouts  0.69 us (5%)
    pallas_call x1, Pallas kernels, shards(): pl.pallas_call(functools.partial(kernel, rows, cols, species), out_shape=...  13.7 us
    unnamed x1, local copies, waits for them, and re-layouts  0.69 us

profile of v3, /device:TPU:1, one launch (start us, length us, event | category | flops | bytes accessed | tf_op | source)
XLA Modules:
  0.0 14.4 jit_solution(17302035057272548867)
XLA Ops:
  0.0 13.7 %shard_map.109 = f32[54,8,128]{2,1,0:T(8,128)S(1)} custom-call(f32[54,8,128]{2,1,0:T(8,128)} %mix_hbm.1, f32[8,128]{1,0:T(8,128)} %diff_hbm.1, f32[2,8,128]{2,1,0:T(8,128)} %speed_hbm.1, f32[8,128]{1,0:T(8,128)} %heat_hbm.1, s32[8,128]{1,0:T(8,128)} %active_hbm.1, bf16[55,256]{1,0:T(8,128)(2,1)} %bitcast.4, bf16[256,256]{1,0:T(8,128)(2,1)} %w2_hbm.1, ...), custom_call_target="tpu_custom_call" | custom-call | tf_op jit(solution)/shard_map/pallas_call | solution.py:309
  13.8 0.7 %copy.13 = f32[54,8,128]{2,1,0:T(8,128)} copy(f32[54,8,128]{2,1,0:T(8,128)S(1)} %shard_map.109) | data formatting | bytes 442368

commit v4 on v3

--- a/solution.py
+++ b/solution.py
@@ -15,6 +15,7 @@
 CHUNKS = 2
 WIDTH = 64
 UNROLL = 1
+PIECE = 4
 MESH_ID = pl.DeviceIdType.MESH
 DIRECTIONS = tuple((dr, dc) for dr in (-1, 0, 1) for dc in (-1, 0, 1) if (dr, dc) != (0, 0))
 
@@ -67,7 +68,7 @@
     b1_hbm, b2_hbm, b3_hbm,
     out_ref,
     b1_ref, b2_ref, b3_ref,
-    field, halo, side, corner, next_c, next_h, adv, heat_v, active_v, w1_v, w2_v, w3_v, w1_p, w2_p, w3_s, w3_p, b3_p, chosen, spread,
+    field, halo, side, corner, weight, joins, adv, heat_v, active_v, w1_v, w2_v, w3_v, w1_p, w2_p, w3_s, w3_p, b3_p, chosen, spread,
     local_sem, send_sem, recv_sem,
 ):
     r, c = lax.axis_index("row"), lax.axis_index("col")
@@ -128,24 +129,40 @@
     row_sides, col_sides = one(r > 0) + one(r < rows - 1), one(c > 0) + one(c < cols - 1)
     pl.semaphore_wait(barrier, (1 + row_sides) * (1 + col_sides) - 1)
 
-    def message(index):
+    pieces = [(packed - GROUP, 2 * GROUP)] + [
+        (GROUP * k, GROUP * min(PIECE, slots - k)) for k in range(0, slots, PIECE)
+    ]
+
+    def message(index, piece=0):
         dr, dc = DIRECTIONS[index]
         strip = {1: pl.ds(5, 3), -1: pl.ds(0, 3), 0: pl.ds(0, 8)}[dr]
         if dc == 0:
-            src, dst = field.at[:, strip, :], halo.at[:, strip, :]
+            some = pl.ds(*pieces[piece])
+            src, dst = field.at[some, strip, :], halo.at[some, strip, :]
         else:
             target = side if dr == 0 else corner
             src = field.at[pl.ds(packed, GROUP), strip, :]
             dst = target.at[pl.ds(0 if dc > 0 else GROUP, GROUP), strip, :]
         return pltpu.make_async_remote_copy(
-            src_ref=src, dst_ref=dst, send_sem=send_sem.at[index], recv_sem=recv_sem.at[index],
+            src_ref=src, dst_ref=dst, send_sem=send_sem.at[index, piece], recv_sem=recv_sem.at[index, piece],
             device_id=(r + dr, c + dc), device_id_type=MESH_ID,
         )
 
-    for index, (dr, dc) in enumerate(DIRECTIONS):
-        @pl.when(there(dr, dc))
-        def _(index=index):
-            message(index).start()
+    def for_each(action, numbers, sign):
+        for number in numbers:
+            for index, (dr, dc) in enumerate(DIRECTIONS):
+                if number and dc:
+                    continue
+
+                @pl.when(there(sign * dr, sign * dc))
+                def _(index=index, number=number):
+                    action(message(index, number))
+
+    def arrive(begin):
+        for_each(lambda m: m.wait_recv(), [1 + begin // PIECE], -1)
+
+    everything = range(len(pieces))
+    for_each(lambda m: m.start(), everything, 1)
 
     for load in loads[3:]:
         load.wait()
@@ -173,10 +190,7 @@
         hit = index == place[q : q + 1]
         chosen[:, 128 * q : 128 * (q + 1)] = jnp.where(hit, 1.0, 0.0).astype(jnp.bfloat16)
 
-    for index, (dr, dc) in enumerate(DIRECTIONS):
-        @pl.when(there(-dr, -dc))
-        def _(index=index):
-            message(index).wait_recv()
+    for_each(lambda m: m.wait_recv(), [0], -1)
 
     own_c, own_h = field[pl.ds(packed, GROUP)], halo[pl.ds(packed, GROUP)]
     lower = in_slot < 3
@@ -224,21 +238,13 @@
     lanes_h = tuple(around_lanes(tile_h[i], join_h[i], slots) for i in range(2))
     wc, wh = weights(*(tile_c[i] for i in range(3)), *(tile_h[i] for i in range(3)), lanes_c, lanes_h, None, in_outer)
 
+    for i in range(5):
+        weight[i] = wc[i]
+        weight[5 + i] = wh[i]
     for step in range(TRANSPORT_STEPS):
-        final = step == TRANSPORT_STEPS - 1
-        for k in range(slots):
-            here = pl.ds(GROUP * k, GROUP)
-            xc, xh = (field[here], halo[here]) if step == 0 else (next_c[here], next_h[here])
-            nc, sc, nh, sh = around_rows(xc, xh, first, last)
-            ec, wcc = around_lanes(xc, join_c, k)
-            new = apply_step(wc, xc, ec, wcc, nc, sc)
-            if final:
-                adv[pl.ds(8 * GROUP * k, 8 * GROUP), :] = new.reshape(8 * GROUP, 128)
-            else:
-                eh, whh = around_lanes(xh, join_h, k)
-                next_c[here] = new
-                next_h[here] = apply_step(wh, xh, eh, whh, nh, sh)
-        if not final:
+        joins[2 * step] = joined(faces[0][0], faces[1][0])
+        joins[2 * step + 1] = joined(faces[0][1], faces[1][1])
+        if step < TRANSPORT_STEPS - 1:
             moved = []
             for (fc, fh), (fwc, fwh) in zip(faces, face_w):
                 nc, sc, nh, sh = around_rows(fc, fh, first, last)
@@ -247,7 +253,24 @@
                     apply_step(fwh, fh, roll_lanes(fh, -1), roll_lanes(fh, 1), nh, sh),
                 ))
             faces = moved
-            join_c, join_h = joined(faces[0][0], faces[1][0]), joined(faces[0][1], faces[1][1])
+
+    def advance_group(k):
+        here = pl.ds(GROUP * k, GROUP)
+        xc, xh = field[here], halo[here]
+        for step in range(TRANSPORT_STEPS):
+            nc, sc, nh, sh = around_rows(xc, xh, first, last)
+            ec, wcc = around_lanes(xc, joins[2 * step], k)
+            new = apply_step([weight[i] for i in range(5)], xc, ec, wcc, nc, sc)
+            if step < TRANSPORT_STEPS - 1:
+                eh, whh = around_lanes(xh, joins[2 * step + 1], k)
+                xh = apply_step([weight[5 + i] for i in range(5)], xh, eh, whh, nh, sh)
+            xc = new
+        adv[pl.ds(8 * GROUP * k, 8 * GROUP), :] = xc.reshape(8 * GROUP, 128)
+
+    for begin in range(0, slots, PIECE):
+        arrive(begin)
+        for k in range(begin, min(begin + PIECE, slots)):
+            advance_group(k)
 
     adv[pl.ds(8 * species, 8), :] = heat_v[...]
     adv[pl.ds(8 * (species + 1), 8 * (WIDTH - species - 1)), :] = jnp.zeros((8 * (WIDTH - species - 1), 128), jnp.float32)
@@ -292,10 +315,7 @@
     for s in range(species):
         out_ref[s] = adv[pl.ds(8 * s, 8), :] + spread[pl.ds(s, 8, stride=WIDTH), :]
 
-    for index, (dr, dc) in enumerate(DIRECTIONS):
-        @pl.when(there(dr, dc))
-        def _(index=index):
-            message(index).wait_send()
+    for_each(lambda m: m.wait_send(), everything, 1)
 
 
 def shards(rows, cols, mix, diff, speed, heat, active, w1, b1, w2, b2, w3, b3):
@@ -303,6 +323,7 @@
     padded = pl.cdiv(species, GROUP) * GROUP
     fields = padded + 2 * GROUP
     hidden, features = w1.shape
+    parts = 1 + pl.cdiv(padded // GROUP, PIECE)
     vm = pltpu.VMEM
     f32, bf16 = jnp.float32, jnp.bfloat16
     held = lambda x: pltpu.with_memory_space_constraint(x, pltpu.HBM)
@@ -319,8 +340,8 @@
             vm((fields, height, width), f32),
             vm((2 * GROUP, height, width), f32),
             vm((2 * GROUP, height, width), f32),
-            vm((padded, height, width), f32),
-            vm((padded, height, width), f32),
+            vm((10, height, width), f32),
+            vm((2 * TRANSPORT_STEPS, GROUP, height, width), f32),
             vm((WIDTH * height, width), f32),
             vm((height, width), f32),
             vm((height, width), jnp.int32),
@@ -335,8 +356,8 @@
             vm((3 * (height * width // 8), height * width), bf16),
             vm((WIDTH * height, width), f32),
             pltpu.SemaphoreType.DMA((11,)),
-            pltpu.SemaphoreType.DMA((8,)),
-            pltpu.SemaphoreType.DMA((8,)),
+            pltpu.SemaphoreType.DMA((8, parts)),
+            pltpu.SemaphoreType.DMA((8, parts)),
         ],
         compiler_params=pltpu.CompilerParams(collective_id=0, has_side_effects=True, vmem_limit_bytes=16 << 20),
     )(*(held(x) for x in (mix, diff, speed, heat, active, w1.T, w2, w3, b1[None], b2[None], b3[None])))

time: 14.6 us -> 15.2 us (1.041)
  Pallas kernels: 13.7 us -> 14.4 us
    pallas_call x1, Pallas kernels: 13.7 us -> 14.4 us  [shards(): pl.pallas_call(functools.partial(kernel, rows, cols, species), out_shape=...]
where the time goes in v4:
time: 15.2 us; the launch traced here: 15.1 us
  Pallas kernels  14.4 us (95%)
  local copies, waits for them, and re-layouts  0.69 us (5%)
    pallas_call x1, Pallas kernels, shards(): pl.pallas_call(functools.partial(kernel, rows, cols, species), out_shape=...  14.4 us
    unnamed x1, local copies, waits for them, and re-layouts  0.69 us

profile of v4, /device:TPU:1, one launch (start us, length us, event | category | flops | bytes accessed | tf_op | source)
XLA Modules:
  0.0 15.1 jit_solution(11641993065498743623)
XLA Ops:
  0.0 14.4 %shard_map.109 = f32[54,8,128]{2,1,0:T(8,128)S(1)} custom-call(f32[54,8,128]{2,1,0:T(8,128)} %mix_hbm.1, f32[8,128]{1,0:T(8,128)} %diff_hbm.1, f32[2,8,128]{2,1,0:T(8,128)} %speed_hbm.1, f32[8,128]{1,0:T(8,128)} %heat_hbm.1, s32[8,128]{1,0:T(8,128)} %active_hbm.1, bf16[55,256]{1,0:T(8,128)(2,1)} %bitcast.4, bf16[256,256]{1,0:T(8,128)(2,1)} %w2_hbm.1, ...), custom_call_target="tpu_custom_call" | custom-call | tf_op jit(solution)/shard_map/pallas_call | solution.py:330
  14.4 0.7 %copy.13 = f32[54,8,128]{2,1,0:T(8,128)} copy(f32[54,8,128]{2,1,0:T(8,128)S(1)} %shard_map.109) | data formatting | bytes 442368

commit v5 on v4

--- a/solution.py
+++ b/solution.py
@@ -14,8 +14,8 @@
 SLOT = 8
 CHUNKS = 2
 WIDTH = 64
-UNROLL = 1
-PIECE = 4
+UNROLL = 4
+PIECE = 7
 MESH_ID = pl.DeviceIdType.MESH
 DIRECTIONS = tuple((dr, dc) for dr in (-1, 0, 1) for dc in (-1, 0, 1) if (dr, dc) != (0, 0))
 
@@ -135,6 +135,7 @@
 
     def message(index, piece=0):
         dr, dc = DIRECTIONS[index]
+        number = index if piece == 0 else 6 + 2 * piece + (dr + 1) // 2
         strip = {1: pl.ds(5, 3), -1: pl.ds(0, 3), 0: pl.ds(0, 8)}[dr]
         if dc == 0:
             some = pl.ds(*pieces[piece])
@@ -144,7 +145,7 @@
             src = field.at[pl.ds(packed, GROUP), strip, :]
             dst = target.at[pl.ds(0 if dc > 0 else GROUP, GROUP), strip, :]
         return pltpu.make_async_remote_copy(
-            src_ref=src, dst_ref=dst, send_sem=send_sem.at[index, piece], recv_sem=recv_sem.at[index, piece],
+            src_ref=src, dst_ref=dst, send_sem=send_sem.at[number], recv_sem=recv_sem.at[number],
             device_id=(r + dr, c + dc), device_id_type=MESH_ID,
         )
 
@@ -168,12 +169,17 @@
         load.wait()
     w1_p[...] = jnp.zeros_like(w1_p)
     w1_p[pl.ds(0, species + 1), :] = w1_v[...]
+    rest = b1_ref[...]
+    for i in range(3):
+        term = rest.astype(jnp.bfloat16)
+        w1_p[pl.ds(species + 1 + i, 1), :] = term
+        rest = rest - term.astype(jnp.float32)
     w2_p[...] = jnp.transpose(w2_v[...].astype(jnp.float32)).astype(jnp.bfloat16)
     w3_s[...] = jnp.zeros_like(w3_s)
     w3_s[pl.ds(0, species), :] = w3_v[...]
-    w3_p[...] = jnp.transpose(w3_s[...].astype(jnp.float32)).astype(jnp.bfloat16)
+    w3_p[...] = jnp.transpose(CHEM_STEP * w3_s[...].astype(jnp.float32)).astype(jnp.bfloat16)
     b3_p[...] = jnp.zeros_like(b3_p)
-    b3_p[:, pl.ds(0, species)] = b3_ref[...]
+    b3_p[:, pl.ds(0, species)] = CHEM_STEP * b3_ref[...]
 
     capacity = chosen.shape[0]
     flags = jnp.where(active_v[...] == 1, 1.0, 0.0)
@@ -273,7 +279,8 @@
             advance_group(k)
 
     adv[pl.ds(8 * species, 8), :] = heat_v[...]
-    adv[pl.ds(8 * (species + 1), 8 * (WIDTH - species - 1)), :] = jnp.zeros((8 * (WIDTH - species - 1), 128), jnp.float32)
+    adv[pl.ds(8 * (species + 1), 24), :] = jnp.ones((24, 128), jnp.float32)
+    adv[pl.ds(8 * (species + 4), 8 * (WIDTH - species - 4)), :] = jnp.zeros((8 * (WIDTH - species - 4), 128), jnp.float32)
     gathered = None
     for p in range(4):
         x = jnp.concatenate([adv[pl.ds(2 * p + j, WIDTH, stride=8), :] for j in range(2)], axis=1)
@@ -290,20 +297,18 @@
     state = gathered[:, :128] + roll_lanes(gathered[:, :128], WIDTH) + low
     chunk = capacity // CHUNKS
     bases = [state[chunk * i : chunk * (i + 1)] for i in range(CHUNKS)]
-    bias1, bias2, bias3 = b1_ref[...], b2_ref[...], b3_p[...]
-
-    def substep(_, totals):
-        hs = [(base + CHEM_STEP * total).astype(jnp.bfloat16) for base, total in zip(bases, totals)]
-        hs = [jnp.dot(x, w1_p[...], preferred_element_type=jnp.float32) for x in hs]
-        hs = [jnp.tanh(h + bias1).astype(jnp.bfloat16) for h in hs]
+    bias2, bias3 = b2_ref[...], b3_p[...]
+
+    def substep(_, states):
+        hs = [jnp.dot(x.astype(jnp.bfloat16), w1_p[...], preferred_element_type=jnp.float32) for x in states]
+        hs = [jnp.tanh(h).astype(jnp.bfloat16) for h in hs]
         hs = [jnp.dot(h, w2_p[...], preferred_element_type=jnp.float32) for h in hs]
         hs = [jnp.tanh(h + bias2).astype(jnp.bfloat16) for h in hs]
         hs = [jnp.dot(h, w3_p[...], preferred_element_type=jnp.float32) for h in hs]
-        return tuple(total + (h + bias3) for total, h in zip(totals, hs))
-
-    totals = tuple(jnp.zeros_like(b) for b in bases)
-    totals = lax.fori_loop(0, SUBSTEPS, substep, totals, unroll=UNROLL)
-    total = CHEM_STEP * jnp.transpose(jnp.concatenate(totals, axis=0))[:WIDTH]
+        return tuple(x + (h + bias3) for x, h in zip(states, hs))
+
+    states = lax.fori_loop(0, SUBSTEPS, substep, tuple(bases), unroll=UNROLL)
+    total = jnp.transpose(jnp.concatenate([x - base for x, base in zip(states, bases)], axis=0))[:WIDTH]
     high = total.astype(jnp.bfloat16)
     low = (total - high.astype(jnp.float32)).astype(jnp.bfloat16)
     both = jnp.concatenate([high, low], axis=0)
@@ -356,8 +361,8 @@
             vm((3 * (height * width // 8), height * width), bf16),
             vm((WIDTH * height, width), f32),
             pltpu.SemaphoreType.DMA((11,)),
-            pltpu.SemaphoreType.DMA((8, parts)),
-            pltpu.SemaphoreType.DMA((8, parts)),
+            pltpu.SemaphoreType.DMA((6 + 2 * parts,)),
+            pltpu.SemaphoreType.DMA((6 + 2 * parts,)),
         ],
         compiler_params=pltpu.CompilerParams(collective_id=0, has_side_effects=True, vmem_limit_bytes=16 << 20),
     )(*(held(x) for x in (mix, diff, speed, heat, active, w1.T, w2, w3, b1[None], b2[None], b3[None])))

time: 15.2 us -> 14.1 us (0.928)
  Pallas kernels: 14.4 us -> 13.2 us
    pallas_call x1, Pallas kernels: 14.4 us -> 13.2 us  [shards(): pl.pallas_call(functools.partial(kernel, rows, cols, species), out_shape=...]
where the time goes in v5:
time: 14.1 us; the launch traced here: 13.9 us
  Pallas kernels  13.2 us (94%)
  local copies, waits for them, and re-layouts  0.69 us (5%)
    pallas_call x1, Pallas kernels, shards(): pl.pallas_call(functools.partial(kernel, rows, cols, species), out_shape=...  13.2 us
    unnamed x1, local copies, waits for them, and re-layouts  0.69 us

profile of v5, /device:TPU:1, one launch (start us, length us, event | category | flops | bytes accessed | tf_op | source)
XLA Modules:
  0.0 13.9 jit_solution(15550871055716366954)
XLA Ops:
  0.0 13.2 %shard_map.109 = f32[54,8,128]{2,1,0:T(8,128)S(1)} custom-call(f32[54,8,128]{2,1,0:T(8,128)} %mix_hbm.1, f32[8,128]{1,0:T(8,128)} %diff_hbm.1, f32[2,8,128]{2,1,0:T(8,128)} %speed_hbm.1, f32[8,128]{1,0:T(8,128)} %heat_hbm.1, s32[8,128]{1,0:T(8,128)} %active_hbm.1, bf16[55,256]{1,0:T(8,128)(2,1)} %bitcast.4, bf16[256,256]{1,0:T(8,128)(2,1)} %w2_hbm.1, ...), custom_call_target="tpu_custom_call" | custom-call | tf_op jit(solution)/shard_map/pallas_call | solution.py:335
  13.3 0.7 %copy.13 = f32[54,8,128]{2,1,0:T(8,128)} copy(f32[54,8,128]{2,1,0:T(8,128)S(1)} %shard_map.109) | data formatting | bytes 442368
